TPU v7x, 32 devices: a whole 2x2x4 slice. The times are simulated.
32 devices in a mesh: range: 16 (over z, y, x), chip: 2 (over core).
Axes of the slice: x: 2, y: 2, z: 4, core: 2. Of those that a mesh axis runs over, the one named last changes fastest.
Arguments:
- mode_tables: bfloat16 [32, 2048, 768], P('range', None, 'chip'), may hold values from -1 to 1
- attenuation: float32 [32, 768], P('range'), may hold values from 0 to 1, as said below
- excitation: float32 [768, 128], replicated, may hold values from -6 to 6
Outputs:
- fields: float32 [32, 2048, 128], P('range', 'chip')
Inputs may be any that keep to these rules, and one draw needn't show every extreme that they name: attenuation rates, positive.
All inputs are finite; a program needn't handle non-finite values.
Results may differ from a plain program's by a relative error of at most 0.0029.
Values may be sent and summed in bfloat16 or wider, within the bound.
A program may use at most 64 MiB of HBM per device.

v0:
```python
import jax
import jax.numpy as jnp
from jax import lax
from jax.sharding import PartitionSpec as P

highest = lax.Precision.HIGHEST


def from_behind(value, axis, steps):
    count = lax.axis_size(axis)
    initial, last = (max(0, -steps), min(count, count - steps))
    return lax.ppermute(value, axis, [(source, source + steps) for source in range(initial, last)])


def on_device(mode_tables, attenuation, excitation):
    seg_local, height_count, half_count = mode_tables.shape
    chip_count = lax.axis_size("chip")
    count_of_modes = half_count * chip_count
    range_count = lax.axis_size("range")
    position = lax.axis_index("range")
    core_index = lax.axis_index("chip")
    is_first = position == 0
    column_start = core_index * half_count
    identity = jnp.eye(count_of_modes, dtype=jnp.float32)
    damping = jnp.exp(-attenuation)
    earlier_half = from_behind(mode_tables[seg_local - 1], "range", 1)
    tables, earlier = (
        lax.all_gather(mode_tables, "chip", axis=2, tiled=True),
        lax.all_gather(earlier_half, "chip", axis=1, tiled=True),
    )
    previous = jnp.concatenate([earlier[None], tables[:-1]], axis=0)
    intersection = jnp.einsum("shm,shn->smn", tables, previous, preferred_element_type=jnp.float32)
    intersection = intersection.at[0].set(jnp.where(is_first, identity, intersection[0]))
    matrices = damping[:, :, None] * intersection
    prefix = lax.dynamic_slice_in_dim(matrices[0], column_start, half_count, 1)
    segment = 1
    prefix = jnp.dot(matrices[segment], prefix, precision=highest)
    rounds = (range_count - 1).bit_length()
    for level_index in range(rounds):
        distance = 2**level_index
        earlier_part = from_behind(prefix, "range", distance)
        product = jnp.dot(
            lax.all_gather(prefix, "chip", axis=1, tiled=True), earlier_part, precision=highest
        )
        prefix = jnp.where(position >= distance, product, prefix)
    source_rows = lax.dynamic_slice_in_dim(excitation, column_start, half_count, 0)
    reached = lax.psum(jnp.dot(prefix, source_rows, precision=highest), "chip")
    arriving = from_behind(reached, "range", 1)
    amplitude = jnp.where(is_first, excitation, arriving)
    stored = []
    segment = 0
    amplitude = jnp.dot(matrices[segment], amplitude, precision=highest)
    stored.append(amplitude.astype(jnp.bfloat16))
    stored.append(reached.astype(jnp.bfloat16))
    rounded = jnp.stack(stored)
    row_count = height_count // chip_count
    own_rows = lax.dynamic_slice_in_dim(tables, core_index * row_count, row_count, 1)
    return jnp.einsum("shm,smc->shc", own_rows, rounded, preferred_element_type=jnp.float32)


def solution(mesh):
    placed = (P("range", None, "chip"), P("range", None), P())
    return jax.shard_map(
        on_device, mesh=mesh, in_specs=placed, out_specs=P("range", "chip", None), check_vma=False
    )
```

profile of v0, /device:TPU:8, one launch (start us, length us, event | category | flops | bytes accessed | tf_op | source)
XLA Modules:
  0.0 304.3 jit_solution(1678558240698443344)
XLA Ops:
  6.5 0.0 copy-start.1
  6.5 0.0 all-gather.7.cloned.1.call-start
  6.5 0.7 all-gather.7.cloned.1.call-update
  7.3 0.0 copy-start.4
  7.3 0.0 all-gather.9.cloned.1.call-start
  7.3 1.1 copy-done.1
  8.4 0.2 slice_bitcast_fusion.2
  8.6 3.4 %collective-permute-start = (bf16[2048,384]{1,0:T(8,128)(2,1)S(1)}, bf16[2048,384]{1,0:T(8,128)(2,1)S(1)}, u32[]{:S(2)}, u32[]{:S(2)}) collective-permute-start(bf16[2048,384]{1,0:T(8,128)(2,1)S(1)} %slice_bitcast_fusion.2), channel_id=1, source_target_pairs={{0,2},{2,4},{4,6},{6,8},{8,10},{10,12},{12,14},{14,16},{16,18},{18... | collective-permute-start | bytes 4718600 | tf_op jit(solution)/shard_map/ppermute | solution.py:12
  12.0 36.4 %collective-permute-done = bf16[2048,384]{1,0:T(8,128)(2,1)S(1)} collective-permute-done((bf16[2048,384]{1,0:T(8,128)(2,1)S(1)}, bf16[2048,384]{1,0:T(8,128)(2,1)S(1)}, u32[]{:S(2)}, u32[]{:S(2)}) %collective-permute-start) | collective-permute-done | bytes 1572896 | tf_op jit(solution)/shard_map/ppermute | solution.py:12
  48.4 0.0 copy-start.2
  48.4 1.1 copy-done.2
  49.6 0.0 all-gather.9.cloned.1.call-update
  49.6 0.0 all-gather.11.cloned.1.call-start
  49.6 0.0 copy-done.4
  49.7 0.0 all-gather.7.cloned.1.call-done
  49.7 0.0 slice-start
  49.7 11.7 %all-gather.9.cloned.1.call-done = bf16[2048,768]{1,0:T(8,128)(2,1)} async-done(((bf16[2048,384]{1,0:T(8,128)(2,1)}), bf16[2048,768]{1,0:T(8,128)(2,1)}) %all-gather.9.cloned.1.call-update) | async-done | bytes 3145744 | tf_op jit(solution)/shard_map/all_gather | solution.py:29
  61.4 0.0 slice-done
  61.4 9.8 %fusion.10 = f32[2,768,768]{1,2,0:T(8,128)S(1)} fusion(bf16[2,2048,768]{2,1,0:T(8,128)(2,1)} %all-gather.7.cloned.1.call-done, bf16[1,2048,768]{2,1,0:T(8,128)(2,1)S(1)} %slice-done, bf16[1,2048,768]{2,1,0:T(8,128)(2,1)} %bitcast.32), kind=kOutput, calls=%fused_computation.14 | convolution fusion | flops 4834983936 | bytes 17301504 | tf_op jit(solution)/shard_map/shm,shn->smn/dot_general | solution.py:32
  71.2 0.4 fusion.7
  71.6 0.3 broadcast_multiply_fusion
  71.9 0.0 copy-start
  72.0 0.2 slice.43
  72.1 2.1 copy-done
  74.2 8.7 %fusion.6 = f32[768,384]{1,0:T(8,128)} fusion(f32[2,768,768]{1,2,0:T(8,128)S(1)} %broadcast_multiply_fusion, f32[1,768,768]{1,2,0:T(8,128)S(1)} %slice.43, s32[]{:T(128)S(6)} %select_n.58), kind=kOutput, calls=%fused_computation.7 | convolution fusion | flops 2717908992 | bytes 4718596 | tf_op jit(solution)/shard_map/dot_general | solution.py:37
  82.9 0.0 all-gather.11.cloned.1.call-update
  82.9 0.0 all-gather.13.cloned.1.call-start
  83.0 3.4 %collective-permute-start.1 = (f32[768,384]{1,0:T(8,128)}, f32[768,384]{1,0:T(8,128)S(1)}, u32[]{:S(2)}, u32[]{:S(2)}) collective-permute-start(f32[768,384]{1,0:T(8,128)} %fusion.6), channel_id=1, source_target_pairs={{0,2},{2,4},{4,6},{6,8},{8,10},{10,12},{12,14},{14,16},{16,18},{18... | collective-permute-start | bytes 3538952 | tf_op jit(solution)/shard_map/ppermute | solution.py:12
  86.4 28.7 %collective-permute-done.1 = f32[768,384]{1,0:T(8,128)S(1)} collective-permute-done((f32[768,384]{1,0:T(8,128)}, f32[768,384]{1,0:T(8,128)S(1)}, u32[]{:S(2)}, u32[]{:S(2)}) %collective-permute-start.1) | collective-permute-done | bytes 1179680 | tf_op jit(solution)/shard_map/ppermute | solution.py:12
  115.0 0.0 all-gather.11.cloned.1.call-done
  115.0 6.5 %convolution_select_fusion.3 = f32[768,384]{1,0:T(8,128)} fusion(f32[768,384]{1,0:T(8,128)} %fusion.6, f32[768,768]{1,0:T(8,128)} %all-gather.11.cloned.1.call-done, f32[768,384]{1,0:T(8,128)S(1)} %collective-permute-done.1, pred[]{:T(512)S(6)} %ge.15), kind=kOutput, calls=%fused_computation.19 | convolution fusion | flops 2718203904 | bytes 5898241 | tf_op jit(solution)/shard_map/dot_general | solution.py:42
  121.6 0.0 all-gather.13.cloned.1.call-update
  121.6 0.0 all-gather.15.cloned.1.call-start
  121.7 2.5 collective-permute-start.2
  124.2 27.8 %collective-permute-done.2 = f32[768,384]{1,0:T(8,128)S(1)} collective-permute-done((f32[768,384]{1,0:T(8,128)}, f32[768,384]{1,0:T(8,128)S(1)}, u32[]{:S(2)}, u32[]{:S(2)}) %collective-permute-start.2) | collective-permute-done | bytes 1179680 | tf_op jit(solution)/shard_map/ppermute | solution.py:12
  152.0 0.0 all-gather.13.cloned.1.call-done
  152.0 6.5 %convolution_select_fusion.2 = f32[768,384]{1,0:T(8,128)} fusion(f32[768,384]{1,0:T(8,128)} %convolution_select_fusion.3, f32[768,768]{1,0:T(8,128)} %all-gather.13.cloned.1.call-done, f32[768,384]{1,0:T(8,128)S(1)} %collective-permute-done.2, pred[]{:T(512)S(6)} %ge.14), kind=kOutput, calls=%fused_computation.18 | convolution fusion | flops 2718203904 | bytes 5898241 | tf_op jit(solution)/shard_map/dot_general | solution.py:42
  158.5 0.0 all-gather.15.cloned.1.call-update
  158.5 0.0 all-gather.17.cloned.1.call-start
  158.6 3.4 %collective-permute-start.3 = (f32[768,384]{1,0:T(8,128)}, f32[768,384]{1,0:T(8,128)S(1)}, u32[]{:S(2)}, u32[]{:S(2)}) collective-permute-start(f32[768,384]{1,0:T(8,128)} %convolution_select_fusion.2), channel_id=1, source_target_pairs={{0,8},{2,10},{4,12},{6,14},{8,16},{10,18},{12,20},{14,22},{16,24},... | collective-permute-start | bytes 3538952 | tf_op jit(solution)/shard_map/ppermute | solution.py:12
  162.0 25.2 %collective-permute-done.3 = f32[768,384]{1,0:T(8,128)S(1)} collective-permute-done((f32[768,384]{1,0:T(8,128)}, f32[768,384]{1,0:T(8,128)S(1)}, u32[]{:S(2)}, u32[]{:S(2)}) %collective-permute-start.3) | collective-permute-done | bytes 1179680 | tf_op jit(solution)/shard_map/ppermute | solution.py:12
  187.1 0.0 all-gather.15.cloned.1.call-done
  187.1 6.5 %convolution_select_fusion.1 = f32[768,384]{1,0:T(8,128)} fusion(f32[768,384]{1,0:T(8,128)} %convolution_select_fusion.2, f32[768,768]{1,0:T(8,128)} %all-gather.15.cloned.1.call-done, f32[768,384]{1,0:T(8,128)S(1)} %collective-permute-done.3, pred[]{:T(512)S(6)} %ge.13), kind=kOutput, calls=%fused_computation.17 | convolution fusion | flops 2718203904 | bytes 5898241 | tf_op jit(solution)/shard_map/dot_general | solution.py:42
  193.7 0.0 all-gather.17.cloned.1.call-update
  193.7 0.0 all-reduce.2.cloned.1.call-start
  193.8 4.6 %collective-permute-start.4 = (f32[768,384]{1,0:T(8,128)}, f32[768,384]{1,0:T(8,128)S(1)}, u32[]{:S(2)}, u32[]{:S(2)}) collective-permute-start(f32[768,384]{1,0:T(8,128)} %convolution_select_fusion.1), channel_id=1, source_target_pairs={{0,16},{2,18},{4,20},{6,22},{8,24},{10,26},{12,28},{14,30},{1,17},... | collective-permute-start | bytes 3538952 | tf_op jit(solution)/shard_map/ppermute | solution.py:12
  198.3 0.0 copy-start.3
  198.4 48.4 %collective-permute-done.4 = f32[768,384]{1,0:T(8,128)S(1)} collective-permute-done((f32[768,384]{1,0:T(8,128)}, f32[768,384]{1,0:T(8,128)S(1)}, u32[]{:S(2)}, u32[]{:S(2)}) %collective-permute-start.4) | collective-permute-done | bytes 1179680 | tf_op jit(solution)/shard_map/ppermute | solution.py:12
  246.7 0.0 all-gather.17.cloned.1.call-done
  246.7 5.8 %convolution_select_fusion = f32[768,384]{1,0:T(8,128)S(1)} fusion(f32[768,384]{1,0:T(8,128)} %convolution_select_fusion.1, f32[768,768]{1,0:T(8,128)} %all-gather.17.cloned.1.call-done, f32[768,384]{1,0:T(8,128)S(1)} %collective-permute-done.4, pred[]{:T(512)S(6)} %ge.12), kind=kOutput, calls=%fused_computation.16 | convolution fusion | flops 2718203904 | bytes 5898241 | tf_op jit(solution)/shard_map/dot_general | solution.py:42
  252.6 0.0 copy-done.3
  252.6 1.9 fusion.25
  254.5 0.0 all-reduce.2.cloned.1.call-update
  254.5 18.5 %all-reduce.2.cloned.1.call-done = f32[768,128]{1,0:T(8,128)} async-done(((f32[768,128]{1,0:T(8,128)}), f32[768,128]{1,0:T(8,128)}) %all-reduce.2.cloned.1.call-update) | async-done | bytes 393232 | tf_op jit(solution)/shard_map/psum | solution.py:47
  273.0 3.4 %collective-permute-start.5 = (f32[768,128]{1,0:T(8,128)}, f32[768,128]{1,0:T(8,128)S(1)}, u32[]{:S(2)}, u32[]{:S(2)}) collective-permute-start(f32[768,128]{1,0:T(8,128)} %all-reduce.2.cloned.1.call-done), channel_id=1, source_target_pairs={{0,2},{2,4},{4,6},{6,8},{8,10},{10,12},{12,14},{14,16},{16,18},{18... | collective-permute-start | bytes 1179656 | tf_op jit(solution)/shard_map/ppermute | solution.py:12
  276.4 1.0 convert_bitcast_fusion
  277.4 10.8 %collective-permute-done.5 = f32[768,128]{1,0:T(8,128)S(1)} collective-permute-done((f32[768,128]{1,0:T(8,128)}, f32[768,128]{1,0:T(8,128)S(1)}, u32[]{:S(2)}, u32[]{:S(2)}) %collective-permute-start.5) | collective-permute-done | bytes 393248 | tf_op jit(solution)/shard_map/ppermute | solution.py:12
  288.2 5.5 %fusion.18 = bf16[1,768,128]{2,1,0:T(8,128)(2,1)S(1)} fusion(f32[768,128]{1,0:T(8,128)S(1)} %copy-done.3, f32[768,128]{1,0:T(8,128)S(1)} %collective-permute-done.5, pred[]{:T(512)S(6)} %eq.11, f32[2,768,768]{1,2,0:T(8,128)} %copy-done), kind=kOutput, calls=%fused_computation.23 | convolution fusion | flops 906166272 | bytes 3342337 | tf_op jit(solution)/shard_map/dot_general | solution.py:52
  293.6 3.9 %fusion.4 = f32[2,1024,128]{2,1,0:T(8,128)} fusion(bf16[2,2048,768]{2,1,0:T(8,128)(2,1)} %all-gather.7.cloned.1.call-done, s32[]{:T(128)S(6)} %select_n.50, bf16[1,768,128]{2,1,0:T(8,128)(2,1)S(1)} %convert_bitcast_fusion, bf16[1,768,128]{2,1,0:T(8,128)(2,1)S(1)} %fusion.18), kind=kOutput, calls=%fused_computation.4 | convolution fusion | flops 402849792 | bytes 4587524 | tf_op jit(solution)/shard_map/shm,smc->shc/dot_general | solution.py:58
  (1 shorter events, 0.0 us)
Async XLA Ops:
  6.5 1.9 copy-start.1
  6.5 43.2 %all-gather.7.cloned.1.call-start = ((), (), s32[]{:S(2)}) async-start(), calls=%async_computation | async-start | bytes 9437184 | tf_op jit(solution)/shard_map/all_gather | solution.py:28
  7.3 42.4 %copy-start.4 = (f32[2,768]{1,0:T(2,128)S(1)}, f32[2,768]{1,0:T(2,128)}, u32[]{:S(2)}) copy-start(f32[2,768]{1,0:T(2,128)} %param.6) | copy-start | bytes 18436
  7.3 54.1 %all-gather.9.cloned.1.call-start = ((), (), s32[]{:S(2)}) async-start(), calls=%async_computation.1 | async-start | bytes 4718592 | tf_op jit(solution)/shard_map/all_gather | solution.py:29
  8.6 39.8 %collective-permute-start = (bf16[2048,384]{1,0:T(8,128)(2,1)S(1)}, bf16[2048,384]{1,0:T(8,128)(2,1)S(1)}, u32[]{:S(2)}, u32[]{:S(2)}) collective-permute-start(bf16[2048,384]{1,0:T(8,128)(2,1)S(1)} %slice_bitcast_fusion.2), channel_id=1, source_target_pairs={{0,2},{2,4},{4,6},{6,8},{8,10},{10,12},{12,14},{14,16},{16,18},{18... | collective-permute-start | bytes 4718600 | tf_op jit(solution)/shard_map/ppermute | solution.py:12
  48.4 1.1 copy-start.2
  49.6 65.4 %all-gather.11.cloned.1.call-start = ((), (), s32[]{:S(2)}) async-start(), calls=%async_computation.2 | async-start | bytes 3538944 | tf_op jit(solution)/shard_map/all_gather | solution.py:43
  49.7 11.7 %slice-start = ((bf16[2,2048,768]{2,1,0:T(8,128)(2,1)}), bf16[1,2048,768]{2,1,0:T(8,128)(2,1)S(1)}, s32[]{:S(2)}) async-start(bf16[2,2048,768]{2,1,0:T(8,128)(2,1)} %all-gather.7.cloned.1.call-done), calls=%async_computation.7 | async-start | bytes 6291456 | tf_op jit(solution)/shard_map/slice | solution.py:31
  71.9 2.2 copy-start
  82.9 69.0 %all-gather.13.cloned.1.call-start = ((), (), s32[]{:S(2)}) async-start(), calls=%async_computation.3 | async-start | bytes 3538944 | tf_op jit(solution)/shard_map/all_gather | solution.py:43
  83.0 32.1 %collective-permute-start.1 = (f32[768,384]{1,0:T(8,128)}, f32[768,384]{1,0:T(8,128)S(1)}, u32[]{:S(2)}, u32[]{:S(2)}) collective-permute-start(f32[768,384]{1,0:T(8,128)} %fusion.6), channel_id=1, source_target_pairs={{0,2},{2,4},{4,6},{6,8},{8,10},{10,12},{12,14},{14,16},{16,18},{18... | collective-permute-start | bytes 3538952 | tf_op jit(solution)/shard_map/ppermute | solution.py:12
  121.6 65.5 %all-gather.15.cloned.1.call-start = ((), (), s32[]{:S(2)}) async-start(), calls=%async_computation.4 | async-start | bytes 3538944 | tf_op jit(solution)/shard_map/all_gather | solution.py:43
  121.7 30.3 %collective-permute-start.2 = (f32[768,384]{1,0:T(8,128)}, f32[768,384]{1,0:T(8,128)S(1)}, u32[]{:S(2)}, u32[]{:S(2)}) collective-permute-start(f32[768,384]{1,0:T(8,128)} %convolution_select_fusion.3), channel_id=1, source_target_pairs={{0,4},{2,6},{4,8},{6,10},{8,12},{10,14},{12,16},{14,18},{16,20},{1... | collective-permute-start | bytes 3538952 | tf_op jit(solution)/shard_map/ppermute | solution.py:12
  158.5 88.2 %all-gather.17.cloned.1.call-start = ((), (), s32[]{:S(2)}) async-start(), calls=%async_computation.5 | async-start | bytes 3538944 | tf_op jit(solution)/shard_map/all_gather | solution.py:43
  158.6 28.6 %collective-permute-start.3 = (f32[768,384]{1,0:T(8,128)}, f32[768,384]{1,0:T(8,128)S(1)}, u32[]{:S(2)}, u32[]{:S(2)}) collective-permute-start(f32[768,384]{1,0:T(8,128)} %convolution_select_fusion.2), channel_id=1, source_target_pairs={{0,8},{2,10},{4,12},{6,14},{8,16},{10,18},{12,20},{14,22},{16,24},... | collective-permute-start | bytes 3538952 | tf_op jit(solution)/shard_map/ppermute | solution.py:12
  193.7 79.3 %all-reduce.2.cloned.1.call-start = ((), (), s32[]{:S(2)}) async-start(), calls=%async_computation.6 | async-start | bytes 786432 | tf_op jit(solution)/shard_map/psum | solution.py:47
  193.8 53.0 %collective-permute-start.4 = (f32[768,384]{1,0:T(8,128)}, f32[768,384]{1,0:T(8,128)S(1)}, u32[]{:S(2)}, u32[]{:S(2)}) collective-permute-start(f32[768,384]{1,0:T(8,128)} %convolution_select_fusion.1), channel_id=1, source_target_pairs={{0,16},{2,18},{4,20},{6,22},{8,24},{10,26},{12,28},{14,30},{1,17},... | collective-permute-start | bytes 3538952 | tf_op jit(solution)/shard_map/ppermute | solution.py:12
  198.3 54.2 %copy-start.3 = (f32[768,128]{1,0:T(8,128)S(1)}, f32[768,128]{1,0:T(8,128)}, u32[]{:S(2)}) copy-start(f32[768,128]{1,0:T(8,128)} %param.7) | copy-start | bytes 1179652
  273.0 15.2 %collective-permute-start.5 = (f32[768,128]{1,0:T(8,128)}, f32[768,128]{1,0:T(8,128)S(1)}, u32[]{:S(2)}, u32[]{:S(2)}) collective-permute-start(f32[768,128]{1,0:T(8,128)} %all-reduce.2.cloned.1.call-done), channel_id=1, source_target_pairs={{0,2},{2,4},{4,6},{6,8},{8,10},{10,12},{12,14},{14,16},{16,18},{18... | collective-permute-start | bytes 1179656 | tf_op jit(solution)/shard_map/ppermute | solution.py:12
Sparse Core Ops, SparseCore 0:
  8.9 17.9 all-gather.6
  49.7 11.6 all-gather.8
  83.0 12.1 all-gather.10
  121.7 10.3 all-gather.12
  158.7 10.2 all-gather.14
  193.8 10.2 all-gather.16
  254.6 18.3 all-reduce.1
where the time goes:
time: 305 us; the launch traced here: 304 us
  waiting for transfers between devices  208 us (68%)
  matrix products  55.2 us (18%)
  starting transfers between devices  20.8 us (7%)
  between operations  13.7 us (4%)
  local copies, waits for them, and re-layouts  4.66 us (2%)
    ppermute x6, waiting for transfers between devices, from_behind(): lax.ppermute(value, axis, [(source, source + steps) for source in range(i...  177 us
    dot_general x4, matrix products, on_device(): jnp.dot(lax.all_gather(prefix, 'chip', axis=1, tiled=True), earlier_part,...  25.5 us
    ppermute x6, starting transfers between devices, from_behind(): lax.ppermute(value, axis, [(source, source + steps) for source in range(i...  20.6 us
    psum x1, waiting for transfers between devices, on_device(): reached = lax.psum(jnp.dot(prefix, source_rows, precision=highest), 'chip')  18.5 us
    all_gather x1, waiting for transfers between devices, on_device(): lax.all_gather(earlier_half, 'chip', axis=1, tiled=True)  11.7 us
    dot_general x1, matrix products, on_device(): jnp.einsum('shm,shn->smn', tables, previous, preferred_element_type=jnp.f...  9.84 us
    dot_general x1, matrix products, on_device(): prefix = jnp.dot(matrices[segment], prefix, precision=highest)  8.7 us
  transfers between devices with their start and end apart: 13, of which 8 were waited for; matrix products, arithmetic and copies ran while one was open for 0% of the time, Pallas kernels for 0%

commit v1 on v0

--- a/solution.py
+++ b/solution.py
@@ -44,7 +44,9 @@
         )
         prefix = jnp.where(position >= distance, product, prefix)
     source_rows = lax.dynamic_slice_in_dim(excitation, column_start, half_count, 0)
-    reached = lax.psum(jnp.dot(prefix, source_rows, precision=highest), "chip")
+    own = jnp.dot(prefix, source_rows, precision=highest)
+    parts = lax.all_gather(own, "chip")
+    reached = jnp.sum(parts, axis=0)
     arriving = from_behind(reached, "range", 1)
     amplitude = jnp.where(is_first, excitation, arriving)
     stored = []

time: 305 us -> 288 us (0.944)
  waiting for transfers between devices: 208 us -> 192 us
    psum x1 -> x0, waiting for transfers between devices: 18.5 us -> none  [on_device(): reached = lax.psum(jnp.dot(prefix, source_rows, precision=highest), 'chip')]
  transfers between devices with their start and end apart: 13 -> 12, of which waited for: 8 -> 7; matrix products, arithmetic and copies ran while one was open for 0% -> 0% of each run, Pallas kernels for 0% -> 0%
where the time goes in v1:
time: 288 us; the launch traced here: 287 us
  waiting for transfers between devices  192 us (67%)
  matrix products  54.5 us (19%)
  starting transfers between devices  19.4 us (7%)
  between operations  13.7 us (5%)
  local copies, waits for them, and re-layouts  4.65 us (2%)
    ppermute x6, waiting for transfers between devices, from_behind(): lax.ppermute(value, axis, [(source, source + steps) for source in range(i...  179 us
    dot_general x4, matrix products, on_device(): jnp.dot(lax.all_gather(prefix, 'chip', axis=1, tiled=True), earlier_part,...  25.5 us
    ppermute x6, starting transfers between devices, from_behind(): lax.ppermute(value, axis, [(source, source + steps) for source in range(i...  19.2 us
    all_gather x1, waiting for transfers between devices, on_device(): lax.all_gather(earlier_half, 'chip', axis=1, tiled=True)  11.7 us
    dot_general x1, matrix products, on_device(): jnp.einsum('shm,shn->smn', tables, previous, preferred_element_type=jnp.f...  9.85 us
    dot_general x1, matrix products, on_device(): prefix = jnp.dot(matrices[segment], prefix, precision=highest)  8.7 us
  transfers between devices with their start and end apart: 12, of which 7 were waited for; matrix products, arithmetic and copies ran while one was open for 0% of the time, Pallas kernels for 0%

profile of v1, /device:TPU:8, one launch (start us, length us, event | category | flops | bytes accessed | tf_op | source)
XLA Modules:
  0.0 287.2 jit_solution(5376696231832216865)
XLA Ops:
  6.5 0.0 copy-start.1
  6.5 0.0 all-gather.8.cloned.1.call-start
  6.5 0.7 all-gather.8.cloned.1.call-update
  7.3 0.0 copy-start.4
  7.3 0.0 all-gather.10.cloned.1.call-start
  7.3 1.1 copy-done.1
  8.4 0.2 slice_bitcast_fusion.2
  8.6 3.4 %collective-permute-start = (bf16[2048,384]{1,0:T(8,128)(2,1)S(1)}, bf16[2048,384]{1,0:T(8,128)(2,1)S(1)}, u32[]{:S(2)}, u32[]{:S(2)}) collective-permute-start(bf16[2048,384]{1,0:T(8,128)(2,1)S(1)} %slice_bitcast_fusion.2), channel_id=1, source_target_pairs={{0,2},{2,4},{4,6},{6,8},{8,10},{10,12},{12,14},{14,16},{16,18},{18... | collective-permute-start | bytes 4718600 | tf_op jit(solution)/shard_map/ppermute | solution.py:12
  12.0 36.4 %collective-permute-done = bf16[2048,384]{1,0:T(8,128)(2,1)S(1)} collective-permute-done((bf16[2048,384]{1,0:T(8,128)(2,1)S(1)}, bf16[2048,384]{1,0:T(8,128)(2,1)S(1)}, u32[]{:S(2)}, u32[]{:S(2)}) %collective-permute-start) | collective-permute-done | bytes 1572896 | tf_op jit(solution)/shard_map/ppermute | solution.py:12
  48.4 0.0 copy-start.2
  48.4 1.1 copy-done.2
  49.6 0.0 all-gather.10.cloned.1.call-update
  49.6 0.0 all-gather.12.cloned.1.call-start
  49.6 0.0 copy-done.4
  49.7 0.0 all-gather.8.cloned.1.call-done
  49.7 0.0 slice-start
  49.7 11.7 %all-gather.10.cloned.1.call-done = bf16[2048,768]{1,0:T(8,128)(2,1)} async-done(((bf16[2048,384]{1,0:T(8,128)(2,1)}), bf16[2048,768]{1,0:T(8,128)(2,1)}) %all-gather.10.cloned.1.call-update) | async-done | bytes 3145744 | tf_op jit(solution)/shard_map/all_gather | solution.py:29
  61.4 0.0 slice-done
  61.4 9.8 %fusion.10 = f32[2,768,768]{1,2,0:T(8,128)S(1)} fusion(bf16[2,2048,768]{2,1,0:T(8,128)(2,1)} %all-gather.8.cloned.1.call-done, bf16[1,2048,768]{2,1,0:T(8,128)(2,1)S(1)} %slice-done, bf16[1,2048,768]{2,1,0:T(8,128)(2,1)} %bitcast.34), kind=kOutput, calls=%fused_computation.14 | convolution fusion | flops 4834983936 | bytes 17301504 | tf_op jit(solution)/shard_map/shm,shn->smn/dot_general | solution.py:32
  71.2 0.4 fusion.7
  71.6 0.3 broadcast_multiply_fusion
  71.9 0.0 copy-start
  72.0 0.2 slice.43
  72.1 2.1 copy-done
  74.2 8.7 %fusion.6 = f32[768,384]{1,0:T(8,128)} fusion(f32[2,768,768]{1,2,0:T(8,128)S(1)} %broadcast_multiply_fusion, f32[1,768,768]{1,2,0:T(8,128)S(1)} %slice.43, s32[]{:T(128)S(6)} %select_n.58), kind=kOutput, calls=%fused_computation.7 | convolution fusion | flops 2717908992 | bytes 4718596 | tf_op jit(solution)/shard_map/dot_general | solution.py:37
  82.9 0.0 all-gather.12.cloned.1.call-update
  82.9 0.0 all-gather.14.cloned.1.call-start
  83.0 3.4 %collective-permute-start.1 = (f32[768,384]{1,0:T(8,128)}, f32[768,384]{1,0:T(8,128)S(1)}, u32[]{:S(2)}, u32[]{:S(2)}) collective-permute-start(f32[768,384]{1,0:T(8,128)} %fusion.6), channel_id=1, source_target_pairs={{0,2},{2,4},{4,6},{6,8},{8,10},{10,12},{12,14},{14,16},{16,18},{18... | collective-permute-start | bytes 3538952 | tf_op jit(solution)/shard_map/ppermute | solution.py:12
  86.3 28.7 %collective-permute-done.1 = f32[768,384]{1,0:T(8,128)S(1)} collective-permute-done((f32[768,384]{1,0:T(8,128)}, f32[768,384]{1,0:T(8,128)S(1)}, u32[]{:S(2)}, u32[]{:S(2)}) %collective-permute-start.1) | collective-permute-done | bytes 1179680 | tf_op jit(solution)/shard_map/ppermute | solution.py:12
  115.0 0.0 all-gather.12.cloned.1.call-done
  115.0 6.5 %convolution_select_fusion.3 = f32[768,384]{1,0:T(8,128)} fusion(f32[768,384]{1,0:T(8,128)} %fusion.6, f32[768,768]{1,0:T(8,128)} %all-gather.12.cloned.1.call-done, f32[768,384]{1,0:T(8,128)S(1)} %collective-permute-done.1, pred[]{:T(512)S(6)} %ge.15), kind=kOutput, calls=%fused_computation.19 | convolution fusion | flops 2718203904 | bytes 5898241 | tf_op jit(solution)/shard_map/dot_general | solution.py:42
  121.6 0.0 all-gather.14.cloned.1.call-update
  121.6 0.0 all-gather.16.cloned.1.call-start
  121.6 2.5 collective-permute-start.2
  124.1 27.8 %collective-permute-done.2 = f32[768,384]{1,0:T(8,128)S(1)} collective-permute-done((f32[768,384]{1,0:T(8,128)}, f32[768,384]{1,0:T(8,128)S(1)}, u32[]{:S(2)}, u32[]{:S(2)}) %collective-permute-start.2) | collective-permute-done | bytes 1179680 | tf_op jit(solution)/shard_map/ppermute | solution.py:12
  151.9 0.0 all-gather.14.cloned.1.call-done
  151.9 6.5 %convolution_select_fusion.2 = f32[768,384]{1,0:T(8,128)} fusion(f32[768,384]{1,0:T(8,128)} %convolution_select_fusion.3, f32[768,768]{1,0:T(8,128)} %all-gather.14.cloned.1.call-done, f32[768,384]{1,0:T(8,128)S(1)} %collective-permute-done.2, pred[]{:T(512)S(6)} %ge.14), kind=kOutput, calls=%fused_computation.18 | convolution fusion | flops 2718203904 | bytes 5898241 | tf_op jit(solution)/shard_map/dot_general | solution.py:42
  158.5 0.0 all-gather.16.cloned.1.call-update
  158.5 0.0 all-gather.18.cloned.1.call-start
  158.6 3.4 %collective-permute-start.3 = (f32[768,384]{1,0:T(8,128)}, f32[768,384]{1,0:T(8,128)S(1)}, u32[]{:S(2)}, u32[]{:S(2)}) collective-permute-start(f32[768,384]{1,0:T(8,128)} %convolution_select_fusion.2), channel_id=1, source_target_pairs={{0,8},{2,10},{4,12},{6,14},{8,16},{10,18},{12,20},{14,22},{16,24},... | collective-permute-start | bytes 3538952 | tf_op jit(solution)/shard_map/ppermute | solution.py:12
  162.0 25.1 %collective-permute-done.3 = f32[768,384]{1,0:T(8,128)S(1)} collective-permute-done((f32[768,384]{1,0:T(8,128)}, f32[768,384]{1,0:T(8,128)S(1)}, u32[]{:S(2)}, u32[]{:S(2)}) %collective-permute-start.3) | collective-permute-done | bytes 1179680 | tf_op jit(solution)/shard_map/ppermute | solution.py:12
  187.1 0.0 all-gather.16.cloned.1.call-done
  187.1 6.5 %convolution_select_fusion.1 = f32[768,384]{1,0:T(8,128)} fusion(f32[768,384]{1,0:T(8,128)} %convolution_select_fusion.2, f32[768,768]{1,0:T(8,128)} %all-gather.16.cloned.1.call-done, f32[768,384]{1,0:T(8,128)S(1)} %collective-permute-done.3, pred[]{:T(512)S(6)} %ge.13), kind=kOutput, calls=%fused_computation.17 | convolution fusion | flops 2718203904 | bytes 5898241 | tf_op jit(solution)/shard_map/dot_general | solution.py:42
  193.7 0.0 all-gather.18.cloned.1.call-update
  193.7 4.6 %collective-permute-start.4 = (f32[768,384]{1,0:T(8,128)}, f32[768,384]{1,0:T(8,128)S(1)}, u32[]{:S(2)}, u32[]{:S(2)}) collective-permute-start(f32[768,384]{1,0:T(8,128)} %convolution_select_fusion.1), channel_id=1, source_target_pairs={{0,16},{2,18},{4,20},{6,22},{8,24},{10,26},{12,28},{14,30},{1,17},... | collective-permute-start | bytes 3538952 | tf_op jit(solution)/shard_map/ppermute | solution.py:12
  198.3 0.0 copy-start.3
  198.3 48.4 %collective-permute-done.4 = f32[768,384]{1,0:T(8,128)S(1)} collective-permute-done((f32[768,384]{1,0:T(8,128)}, f32[768,384]{1,0:T(8,128)S(1)}, u32[]{:S(2)}, u32[]{:S(2)}) %collective-permute-start.4) | collective-permute-done | bytes 1179680 | tf_op jit(solution)/shard_map/ppermute | solution.py:12
  246.7 0.0 all-gather.18.cloned.1.call-done
  246.7 5.8 %convolution_select_fusion = f32[768,384]{1,0:T(8,128)S(1)} fusion(f32[768,384]{1,0:T(8,128)} %convolution_select_fusion.1, f32[768,768]{1,0:T(8,128)} %all-gather.18.cloned.1.call-done, f32[768,384]{1,0:T(8,128)S(1)} %collective-permute-done.4, pred[]{:T(512)S(6)} %ge.12), kind=kOutput, calls=%fused_computation.16 | convolution fusion | flops 2718203904 | bytes 5898241 | tf_op jit(solution)/shard_map/dot_general | solution.py:42
  252.5 0.0 copy-done.3
  252.5 1.2 fusion.25
  253.7 2.4 all-gather
  256.1 0.1 reduce_sum.9
  256.2 1.9 collective-permute-start.5
  258.1 12.9 %collective-permute-done.5 = f32[768,128]{1,0:T(8,128)S(1)} collective-permute-done((f32[768,128]{1,0:T(8,128)S(1)}, f32[768,128]{1,0:T(8,128)S(1)}, u32[]{:S(2)}, u32[]{:S(2)}) %collective-permute-start.5) | collective-permute-done | bytes 393248 | tf_op jit(solution)/shard_map/ppermute | solution.py:12
  271.0 5.5 %fusion.18 = bf16[1,768,128]{2,1,0:T(8,128)(2,1)S(1)} fusion(f32[768,128]{1,0:T(8,128)S(1)} %copy-done.3, f32[768,128]{1,0:T(8,128)S(1)} %collective-permute-done.5, pred[]{:T(512)S(6)} %eq.11, f32[2,768,768]{1,2,0:T(8,128)} %copy-done), kind=kOutput, calls=%fused_computation.23 | convolution fusion | flops 906166272 | bytes 3342337 | tf_op jit(solution)/shard_map/dot_general | solution.py:54
  276.5 3.9 %fusion.4 = f32[2,1024,128]{2,1,0:T(8,128)} fusion(bf16[2,2048,768]{2,1,0:T(8,128)(2,1)} %all-gather.8.cloned.1.call-done, s32[]{:T(128)S(6)} %select_n.50, bf16[1,768,128]{2,1,0:T(8,128)(2,1)S(1)} %convert_bitcast_fusion, bf16[1,768,128]{2,1,0:T(8,128)(2,1)S(1)} %fusion.18), kind=kOutput, calls=%fused_computation.4 | convolution fusion | flops 402849792 | bytes 4587524 | tf_op jit(solution)/shard_map/shm,smc->shc/dot_general | solution.py:60
  (2 shorter events, 0.0 us)
Async XLA Ops:
  6.5 1.9 copy-start.1
  6.5 43.2 %all-gather.8.cloned.1.call-start = ((), (), s32[]{:S(2)}) async-start(), calls=%async_computation | async-start | bytes 9437184 | tf_op jit(solution)/shard_map/all_gather | solution.py:28
  7.3 42.4 %copy-start.4 = (f32[2,768]{1,0:T(2,128)S(1)}, f32[2,768]{1,0:T(2,128)}, u32[]{:S(2)}) copy-start(f32[2,768]{1,0:T(2,128)} %param.6) | copy-start | bytes 18436
  7.3 54.1 %all-gather.10.cloned.1.call-start = ((), (), s32[]{:S(2)}) async-start(), calls=%async_computation.1 | async-start | bytes 4718592 | tf_op jit(solution)/shard_map/all_gather | solution.py:29
  8.6 39.8 %collective-permute-start = (bf16[2048,384]{1,0:T(8,128)(2,1)S(1)}, bf16[2048,384]{1,0:T(8,128)(2,1)S(1)}, u32[]{:S(2)}, u32[]{:S(2)}) collective-permute-start(bf16[2048,384]{1,0:T(8,128)(2,1)S(1)} %slice_bitcast_fusion.2), channel_id=1, source_target_pairs={{0,2},{2,4},{4,6},{6,8},{8,10},{10,12},{12,14},{14,16},{16,18},{18... | collective-permute-start | bytes 4718600 | tf_op jit(solution)/shard_map/ppermute | solution.py:12
  48.4 1.1 copy-start.2
  49.6 65.4 %all-gather.12.cloned.1.call-start = ((), (), s32[]{:S(2)}) async-start(), calls=%async_computation.2 | async-start | bytes 3538944 | tf_op jit(solution)/shard_map/all_gather | solution.py:43
  49.7 11.7 %slice-start = ((bf16[2,2048,768]{2,1,0:T(8,128)(2,1)}), bf16[1,2048,768]{2,1,0:T(8,128)(2,1)S(1)}, s32[]{:S(2)}) async-start(bf16[2,2048,768]{2,1,0:T(8,128)(2,1)} %all-gather.8.cloned.1.call-done), calls=%async_computation.6 | async-start | bytes 6291456 | tf_op jit(solution)/shard_map/slice | solution.py:31
  71.9 2.2 copy-start
  82.9 69.0 %all-gather.14.cloned.1.call-start = ((), (), s32[]{:S(2)}) async-start(), calls=%async_computation.3 | async-start | bytes 3538944 | tf_op jit(solution)/shard_map/all_gather | solution.py:43
  83.0 32.1 %collective-permute-start.1 = (f32[768,384]{1,0:T(8,128)}, f32[768,384]{1,0:T(8,128)S(1)}, u32[]{:S(2)}, u32[]{:S(2)}) collective-permute-start(f32[768,384]{1,0:T(8,128)} %fusion.6), channel_id=1, source_target_pairs={{0,2},{2,4},{4,6},{6,8},{8,10},{10,12},{12,14},{14,16},{16,18},{18... | collective-permute-start | bytes 3538952 | tf_op jit(solution)/shard_map/ppermute | solution.py:12
  121.6 65.5 %all-gather.16.cloned.1.call-start = ((), (), s32[]{:S(2)}) async-start(), calls=%async_computation.4 | async-start | bytes 3538944 | tf_op jit(solution)/shard_map/all_gather | solution.py:43
  121.6 30.3 %collective-permute-start.2 = (f32[768,384]{1,0:T(8,128)}, f32[768,384]{1,0:T(8,128)S(1)}, u32[]{:S(2)}, u32[]{:S(2)}) collective-permute-start(f32[768,384]{1,0:T(8,128)} %convolution_select_fusion.3), channel_id=1, source_target_pairs={{0,4},{2,6},{4,8},{6,10},{8,12},{10,14},{12,16},{14,18},{16,20},{1... | collective-permute-start | bytes 3538952 | tf_op jit(solution)/shard_map/ppermute | solution.py:12
  158.5 88.2 %all-gather.18.cloned.1.call-start = ((), (), s32[]{:S(2)}) async-start(), calls=%async_computation.5 | async-start | bytes 3538944 | tf_op jit(solution)/shard_map/all_gather | solution.py:43
  158.6 28.6 %collective-permute-start.3 = (f32[768,384]{1,0:T(8,128)}, f32[768,384]{1,0:T(8,128)S(1)}, u32[]{:S(2)}, u32[]{:S(2)}) collective-permute-start(f32[768,384]{1,0:T(8,128)} %convolution_select_fusion.2), channel_id=1, source_target_pairs={{0,8},{2,10},{4,12},{6,14},{8,16},{10,18},{12,20},{14,22},{16,24},... | collective-permute-start | bytes 3538952 | tf_op jit(solution)/shard_map/ppermute | solution.py:12
  193.7 53.0 %collective-permute-start.4 = (f32[768,384]{1,0:T(8,128)}, f32[768,384]{1,0:T(8,128)S(1)}, u32[]{:S(2)}, u32[]{:S(2)}) collective-permute-start(f32[768,384]{1,0:T(8,128)} %convolution_select_fusion.1), channel_id=1, source_target_pairs={{0,16},{2,18},{4,20},{6,22},{8,24},{10,26},{12,28},{14,30},{1,17},... | collective-permute-start | bytes 3538952 | tf_op jit(solution)/shard_map/ppermute | solution.py:12
  198.3 54.2 %copy-start.3 = (f32[768,128]{1,0:T(8,128)S(1)}, f32[768,128]{1,0:T(8,128)}, u32[]{:S(2)}) copy-start(f32[768,128]{1,0:T(8,128)} %param.7) | copy-start | bytes 1179652
  256.2 14.8 %collective-permute-start.5 = (f32[768,128]{1,0:T(8,128)S(1)}, f32[768,128]{1,0:T(8,128)S(1)}, u32[]{:S(2)}, u32[]{:S(2)}) collective-permute-start(f32[768,128]{1,0:T(8,128)S(1)} %reduce_sum.9), channel_id=1, source_target_pairs={{0,2},{2,4},{4,6},{6,8},{8,10},{10,12},{12,14},{14,16},{16,18},{18... | collective-permute-start | bytes 1179656 | tf_op jit(solution)/shard_map/ppermute | solution.py:12
Sparse Core Ops, SparseCore 0:
  8.9 17.9 all-gather.7
  49.7 11.6 all-gather.9
  83.0 12.1 all-gather.11
  121.7 10.3 all-gather.13
  158.6 10.3 all-gather.15
  193.8 10.3 all-gather.17
